TPU v7x, 128 devices: a whole 4x4x4 slice. The times are simulated.
128 devices in a mesh: row: 32 (over x, z, y_lo), loop: 4 (over y_hi, core).
Axes of the slice: x: 4, y: 4 (y_hi: 2, y_lo: 2; y = y_hi * 2 + y_lo), z: 4, core: 2. Of those that a mesh axis runs over, the one named last changes fastest.
Arguments:
- pair: bfloat16 [768, 768, 128], P('row', 'loop'), may hold values from -6 to 6
- ln_in_gain: float32 [128], replicated, may hold values from 0.1 to 1.9
- ln_in_bias: float32 [128], replicated, may hold values from -3 to 3
- w_proj: bfloat16 [128, 512], replicated, may hold values from -0.5 to 0.5
- w_gate: bfloat16 [128, 128], replicated, may hold values from -0.5 to 0.5
- ln_out_gain: float32 [128], replicated, may hold values from 0.1 to 1.9
- ln_out_bias: float32 [128], replicated, may hold values from -3 to 3
- w_out: bfloat16 [128, 128], replicated, may hold values from -0.5 to 0.5
Outputs:
- update: bfloat16 [768, 768, 128], P('row', 'loop')
All inputs are finite; a program needn't handle non-finite values.
Results may differ from a plain program's by a relative error of at most 0.0055.
Values may be sent and summed in bfloat16 or wider, within the bound.
A program may use at most 192 MiB of HBM per device.

v0:
```python
import jax
import jax.numpy as jnp
from jax import lax
from jax.sharding import PartitionSpec as P

epsilon = 1e-05


def layer_norm(values, gain, bias):
    values = values.astype(jnp.float32)
    center = values - jnp.mean(values, axis=-1, keepdims=True)
    spread = jnp.mean(center * center, axis=-1, keepdims=True)
    return center * lax.rsqrt(spread + epsilon) * gain + bias


def gated_pair(flat_normed, weights, hidden):
    projected = jnp.dot(flat_normed, weights, preferred_element_type=jnp.float32)
    return (jax.nn.sigmoid(projected[:, :hidden]) * projected[:, hidden:]).astype(jnp.bfloat16)


def on_device(pair, ln_in_gain, ln_in_bias, w_proj, w_gate, ln_out_gain, ln_out_bias, w_out):
    local_rows, local_cols, channels = pair.shape
    hidden = w_out.shape[0]
    normed = layer_norm(pair, ln_in_gain, ln_in_bias).astype(jnp.bfloat16)
    flat_normed = normed.reshape(local_rows * local_cols, channels)
    left = gated_pair(flat_normed, w_proj[:, : 2 * hidden], hidden).reshape(
        local_rows, local_cols, hidden
    )
    right = gated_pair(flat_normed, w_proj[:, 2 * hidden :], hidden).reshape(
        local_rows, local_cols, hidden
    )
    left_wide = lax.all_gather(left, "loop", axis=1, tiled=True)
    left_t = lax.all_to_all(left_wide, "row", split_axis=1, concat_axis=0, tiled=True)
    left_major = left_t.transpose(2, 1, 0)
    right_major = right.transpose(2, 0, 1)
    triangle_major = lax.dot_general(
        left_major,
        lax.all_gather(right_major, "row", axis=1, tiled=True),
        (((2,), (1,)), ((0,), (0,))),
        preferred_element_type=jnp.float32,
    )
    triangle = triangle_major.transpose(1, 2, 0)
    mixed = layer_norm(triangle, ln_out_gain, ln_out_bias).astype(jnp.bfloat16)
    outgoing = jnp.dot(
        mixed.reshape(local_rows * local_cols, hidden), w_out, preferred_element_type=jnp.float32
    )
    gating = jax.nn.sigmoid(jnp.dot(flat_normed, w_gate, preferred_element_type=jnp.float32))
    return (gating * outgoing).astype(jnp.bfloat16).reshape(local_rows, local_cols, channels)


def solution(mesh):
    return jax.shard_map(
        on_device,
        mesh=mesh,
        in_specs=(P("row", "loop", None), P(), P(), P(), P(), P(), P(), P()),
        out_specs=P("row", "loop", None),
        check_vma=False,
    )
```

profile of v0, /device:TPU:0, one launch (start us, length us, event | category | flops | bytes accessed | tf_op | source)
XLA Modules:
  0.0 1214.2 jit_solution(7628084886338595874)
XLA Ops:
  6.5 0.0 all-gather.3.cloned.1.call-start
  6.6 1.9 convert_reduce_fusion
  8.5 2.8 fusion.8
  11.3 1.5 fusion.11
  12.8 0.8 fusion.22
  13.6 0.6 fusion.16
  14.2 1.8 copy.24
  16.0 0.0 all-gather.5.cloned.1.call-start
  16.0 0.8 fusion.20
  16.8 0.6 fusion.12
  17.4 2.0 copy.28
  19.4 40.7 %all-gather.3.cloned.1.call-done = bf16[24,768,128]{2,0,1:T(8,128)(2,1)} async-done(((bf16[24,192,128]{2,0,1:T(8,128)(2,1)}), bf16[24,768,128]{2,0,1:T(8,128)(2,1)}) %all-gather.3.cloned.1.call-update) | async-done | bytes 4718608 | tf_op jit(solution)/shard_map/all_gather | solution.py:32
  60.1 7.5 all-to-all-start
  67.7 2.2 fusion.2
  69.8 109.3 %all-to-all-done = bf16[24,768,128]{2,0,1:T(8,128)(2,1)} async-done(((bf16[24,768,128]{2,0,1:T(8,128)(2,1)}), bf16[24,768,128]{2,0,1:T(8,128)(2,1)}, u32[]{:S(2)}, u32[]{:S(2)}) %all-to-all-start) | async-done | bytes 4718624 | tf_op jit(solution)/shard_map/all_to_all | solution.py:33
  179.1 5.6 copy.26
  184.7 7.7 copy.27
  192.4 989.9 %all-gather.5.cloned.1.call-done = bf16[128,768,192]{2,1,0:T(8,128)(2,1)} async-done(((bf16[128,24,192]{2,1,0:T(8,128)(2,1)}), bf16[128,768,192]{2,1,0:T(8,128)(2,1)}) %all-gather.5.cloned.1.call-update) | async-done | bytes 37748752 | tf_op jit(solution)/shard_map/all_gather | solution.py:38
  1182.3 19.3 %bitcast_reduce_fusion = (f32[24,192]{1,0:T(8,128)S(1)}, f32[128,24,192]{2,1,0:T(8,128)S(1)}) fusion(bf16[128,768,192]{2,1,0:T(8,128)(2,1)} %all-gather.5.cloned.1.call-done, bf16[768,24,128]{0,1,2:T(8,128)(2,1)} %copy.27), kind=kOutput, calls=%fused_computation.9 | convolution fusion | flops 906554880 | bytes 44845056 | tf_op jit(solution)/shard_map/dot_general | solution.py:36
  1201.7 0.4 multiply_reduce_fusion
  1202.1 0.2 copy-done.7
  1202.3 0.5 add_convert_fusion
  1202.9 1.4 copy.29
  1204.3 3.1 fusion.3
  (23 shorter events, 0.1 us)
Async XLA Ops:
  6.5 61.1 %copy-start = (bf16[128,128]{1,0:T(8,128)(2,1)S(1)}, bf16[128,128]{1,0:T(8,128)(2,1)}, u32[]{:S(2)}) copy-start(bf16[128,128]{1,0:T(8,128)(2,1)} %param.12) | copy-start | bytes 98308
  6.5 4.7 copy-start.2
  6.5 4.7 copy-start.5
  6.5 4.8 copy-start.6
  6.5 6.2 copy-start.3
  6.5 53.6 %all-gather.3.cloned.1.call-start = ((), (), s32[]{:S(2)}) async-start(), calls=%async_computation.1 | async-start | bytes 5898240 | tf_op jit(solution)/shard_map/all_gather | solution.py:32
  16.0 1166.3 %all-gather.5.cloned.1.call-start = ((), (), s32[]{:S(2)}) async-start(), calls=%async_computation.2 | async-start | bytes 51904512 | tf_op jit(solution)/shard_map/all_gather | solution.py:38
  60.1 119.0 %all-to-all-start = ((bf16[24,768,128]{2,0,1:T(8,128)(2,1)}), bf16[24,768,128]{2,0,1:T(8,128)(2,1)}, u32[]{:S(2)}, u32[]{:S(2)}) async-start(bf16[24,768,128]{2,0,1:T(8,128)(2,1)} %all-gather.3.cloned.1.call-done), calls=%async_computation | async-start | bytes 9437184 | tf_op jit(solution)/shard_map/all_to_all | solution.py:33
  1201.7 0.7 copy-start.7
  1201.7 0.7 copy-start.8
  1202.8 1.4 copy-start.4
  1204.2 3.2 copy-start.1
Sparse Core Ops, SparseCore 0:
  16.1 43.9 all-gather.2
  61.8 1120.5 all-gather.4
where the time goes:
time: 1220 us; the launch traced here: 1210 us
  waiting for transfers between devices  1140 us (93%)
  matrix products  26.1 us (2%)
  local copies, waits for them, and re-layouts  18.7 us (2%)
  between operations  13.6 us (1%)
    all_gather x1, waiting for transfers between devices, on_device(): lax.all_gather(right_major, 'row', axis=1, tiled=True)  990 us
    all_to_all x1, waiting for transfers between devices, on_device(): lax.all_to_all(left_wide, 'row', split_axis=1, concat_axis=0, tiled=True)  109 us
    all_gather x1, waiting for transfers between devices, on_device(): left_wide = lax.all_gather(left, 'loop', axis=1, tiled=True)  40.7 us
  transfers between devices with their start and end apart: 3, of which 3 were waited for; matrix products, arithmetic and copies ran while one was open for 2% of the time, Pallas kernels for 0%

commit v1 on v0

v1 whole, which is shorter than its diff:
```python
import functools

import jax
import jax.numpy as jnp
from jax import lax
from jax.experimental import pallas as pl
from jax.experimental.pallas import tpu as pltpu
from jax.sharding import PartitionSpec as P

epsilon = 1e-05
MESH = pl.DeviceIdType.MESH
f32 = jnp.float32
bf16 = jnp.bfloat16
CHIPS = 64
NT = (((1,), (1,)), ((), ()))
TN = (((0,), (0,)), ((), ()))


def normalize(values, gain, bias):
    center = values - jnp.mean(values, axis=-1, keepdims=True)
    spread = jnp.mean(center * center, axis=-1, keepdims=True)
    return center * lax.rsqrt(spread + epsilon) * gain + bias


def project_kernel(pair_ref, gain_ref, bias_ref, w_ref, wg_ref, left_ref, right_ref, gate_ref,
                   wide, tall, major_l, major_r, normed):
    @pl.when(pl.program_id(0) == 0)
    def _():
        flipped = w_ref[...].astype(f32).T.astype(bf16)
        wide[...] = flipped
        for kind in range(4):
            rows = pl.ds(64 * kind, 64)
            tall[rows, 0:128] = flipped[128 * kind:128 * kind + 64]
            tall[rows, 128:256] = flipped[128 * kind + 64:128 * kind + 128]

    gain = gain_ref[...]
    bias = bias_ref[...]
    for k in range(8):
        values = normalize(pair_ref[k].astype(f32), gain, bias).astype(bf16)
        normed[k] = values
        head = values[0:128]
        rest = values[128:192]
        zero = jnp.zeros_like(rest)
        both = jnp.concatenate(
            [jnp.concatenate([rest, zero], axis=1), jnp.concatenate([zero, rest], axis=1)], axis=0
        )
        a = lax.dot_general(wide[...], head, NT, preferred_element_type=f32)
        b = lax.dot_general(tall[...], both, NT, preferred_element_type=f32)
        rows = pl.ds(64 * k, 64)
        for major, at in ((major_l, 0), (major_r, 1)):
            full = jax.nn.sigmoid(a[256 * at:256 * at + 128]) * a[256 * at + 128:256 * at + 256]
            part = jax.nn.sigmoid(b[128 * at:128 * at + 64]) * b[128 * at + 64:128 * at + 128]
            major[0, rows] = full[0:64]
            major[1, rows] = part
            major[2, rows] = full[64:128]
        gate = jnp.dot(values, wg_ref[...], preferred_element_type=f32)
        gate_ref[k] = jax.nn.sigmoid(gate)
    for c in range(CHIPS):
        for part in range(3):
            lanes = pl.ds(128 * part, 128)
            picked = pl.ds(c, 8, stride=64)
            left_ref[c, 0, :, lanes] = major_l[part, picked, :].astype(bf16)
            right_ref[c, 0, :, lanes] = major_r[part, picked, :].astype(bf16)


def project(pair, gain, bias, w_proj, w_gate):
    whole = lambda shape: pl.BlockSpec(shape, lambda i: (0,) * len(shape))
    message = jax.ShapeDtypeStruct((CHIPS, 3, 8, 384), bf16)
    return pl.pallas_call(
        project_kernel,
        name="project",
        grid=(3,),
        out_shape=(message, message, jax.ShapeDtypeStruct((24, 192, 128), f32)),
        in_specs=[
            pl.BlockSpec((8, 192, 128), lambda i: (i, 0, 0)),
            whole((1, 128)), whole((1, 128)), whole((128, 512)), whole((128, 128)),
        ],
        out_specs=(
            pl.BlockSpec((CHIPS, 1, 8, 384), lambda i: (0, i, 0, 0)),
            pl.BlockSpec((CHIPS, 1, 8, 384), lambda i: (0, i, 0, 0)),
            pl.BlockSpec((8, 192, 128), lambda i: (i, 0, 0)),
        ),
        scratch_shapes=[
            pltpu.VMEM((512, 128), bf16),
            pltpu.VMEM((256, 256), bf16),
            pltpu.VMEM((3, 512, 128), f32),
            pltpu.VMEM((3, 512, 128), f32),
            pltpu.VMEM((8, 192, 128), bf16),
        ],
        compiler_params=pltpu.CompilerParams(dimension_semantics=("arbitrary",)),
    )(pair, gain, bias, w_proj, w_gate)


def exchange_kernel(left_ref, right_ref, out_ref, own, other, right, flipped, outgoing,
                    send_l, send_r, send_t, recv_l, recv_r, recv_t, pass_send, pass_recv):
    row = lax.axis_index("row")
    loop = lax.axis_index("loop")
    core = loop % 2
    y_hi = loop // 2
    x = row // 8
    z = (row // 2) % 4
    y = y_hi * 2 + row % 2
    me = y_hi * 32 + row

    def target(o):
        tx = (x + o // 16) % 4
        ty = (y + (o // 4) % 4) % 4
        tz = (z + o % 4) % 4
        t_row = (tx * 4 + tz) * 2 + ty % 2
        return (ty // 2) * 32 + t_row, (t_row, (ty // 2) * 2 + core)

    barrier = pltpu.get_barrier_semaphore()

    def greet(o, carry):
        _, device = target(o)
        pl.semaphore_signal(barrier, inc=1, device_id=device, device_id_type=MESH)
        return carry

    lax.fori_loop(1, CHIPS, greet, 0)
    twin = (row, y_hi * 2 + (1 - core))
    pl.semaphore_signal(barrier, inc=1, device_id=twin, device_id_type=MESH)
    pl.semaphore_wait(barrier, CHIPS)

    def send_all(src, dst, send, recv):
        def body(n, carry):
            chip, device = target((n * 21) % CHIPS)
            pltpu.make_async_remote_copy(
                src.at[chip], dst.at[me], send, recv.at[y_hi], device_id=device, device_id_type=MESH
            ).start()
            return carry

        lax.fori_loop(1, CHIPS, body, 0)
        pltpu.make_async_copy(src.at[me], dst.at[me], recv.at[y_hi]).start()

    send_all(left_ref, own, send_l, recv_l)
    send_all(right_ref, right, send_r, recv_r)

    def half(ref, h):
        return ref.at[pl.ds(h * 32, 32)]

    passed = []
    for h in range(2):
        pltpu.make_async_copy(half(own, h), half(own, h), recv_l.at[h]).wait()
        copy = pltpu.make_async_remote_copy(
            half(own, h), half(other, h), pass_send.at[h], pass_recv.at[h],
            device_id=twin, device_id_type=MESH,
        )
        copy.start()
        passed.append(copy)

    def flip(ref, h, of):
        block = ref[pl.ds(h * 32, 32)].reshape(768, 384)
        flipped[h * 2 + of] = block.T

    for h in range(2):
        flip(own, h, core)
    for h in range(2):
        passed[h].wait()
        flip(other, h, 1 - core)

    for h in range(2):
        pltpu.make_async_copy(half(right, h), half(right, h), recv_r.at[h]).wait()

    lane = lax.broadcasted_iota(jnp.int32, (192, 128), 1)

    def multiply(n, carry):
        h = (y_hi + n // 4) % 2
        block = (x + 2 + n) % 4
        first = h * 32 + block * 8
        r = right[pl.ds(h * 32, 32)].reshape(768, 384)
        l = flipped[block]
        t0 = jnp.dot(l[0:192], r[:, 0:256], preferred_element_type=f32)
        t1 = jnp.dot(l[192:384], r[:, 128:384], preferred_element_type=f32)
        t1 = jnp.concatenate([t1[64:192], t1[0:64]], axis=0)
        mid = jnp.where(lane < 64, t0[:, 128:256], t1[:, 0:128])
        t = jnp.concatenate([t0[:, 0:128], mid, t1[:, 128:256]], axis=1)
        outgoing[pl.ds(first, 8)] = t.reshape(8, 3, 8, 384).astype(bf16)

        def ship(m, inner):
            chip = first + m

            @pl.when(chip != me)
            def _():
                t_row = block * 8 + m
                pltpu.make_async_remote_copy(
                    outgoing.at[chip], out_ref.at[me], send_t, recv_t,
                    device_id=(t_row, h * 2 + core), device_id_type=MESH,
                ).start()

            return inner

        lax.fori_loop(0, 8, ship, 0)
        return carry

    lax.fori_loop(0, 8, multiply, 0)
    pltpu.make_async_copy(outgoing.at[me], out_ref.at[me], recv_t).start()
    pltpu.make_async_copy(outgoing, out_ref, recv_t).wait()
    most = pl.ds(0, CHIPS - 1)
    pltpu.make_async_copy(left_ref.at[most], own.at[most], send_l).wait()
    pltpu.make_async_copy(right_ref.at[most], right.at[most], send_r).wait()
    pltpu.make_async_copy(outgoing.at[most], out_ref.at[most], send_t).wait()


def exchange(left, right):
    message = (CHIPS, 3, 8, 384)
    dma = pltpu.SemaphoreType.DMA
    return pl.pallas_call(
        exchange_kernel,
        name="exchange",
        out_shape=jax.ShapeDtypeStruct(message, bf16),
        in_specs=[pl.BlockSpec(memory_space=pl.ANY)] * 2,
        out_specs=pl.BlockSpec(memory_space=pl.ANY),
        scratch_shapes=[
            pltpu.VMEM(message, bf16),
            pltpu.VMEM(message, bf16),
            pltpu.VMEM(message, bf16),
            pltpu.VMEM((4, 384, 768), bf16),
            pltpu.VMEM(message, bf16),
            dma, dma, dma, dma((2,)), dma((2,)), dma, dma((2,)), dma((2,)),
        ],
        compiler_params=pltpu.CompilerParams(collective_id=0, has_side_effects=True),
    )(left, right)


def finish_kernel(t_ref, gate_ref, gain_ref, bias_ref, w_ref, out_ref, scale, shift, major):
    @pl.when(pl.program_id(0) == 0)
    def _():
        diagonal = (lax.broadcasted_iota(jnp.int32, (128, 128), 0)
                    == lax.broadcasted_iota(jnp.int32, (128, 128), 1))
        lane = lax.broadcasted_iota(jnp.int32, (64, 128), 1)
        for source, dest in ((gain_ref, scale), (bias_ref, shift)):
            column = jnp.sum(jnp.where(diagonal, source[...], 0.0), axis=1, keepdims=True)
            wide = jnp.broadcast_to(column, (128, 128))
            dest[:, 0:128] = wide[0:64]
            dest[:, 128:256] = jnp.where(lane < 64, wide[0:64], wide[64:128])
            dest[:, 256:384] = wide[64:128]

    def over_channels(values):
        total = jnp.sum(values, axis=0)
        ends = total[:, 0:128] + total[:, 256:384]
        mid = total[:, 128:256]
        mid = mid + pltpu.roll(mid, 64, 1)
        return jnp.concatenate([ends, mid, ends], axis=1) * (1.0 / 128)

    t = t_ref[:, 0].astype(f32)
    center = t - over_channels(t)[None]
    spread = over_channels(center * center)
    scaled = (center * lax.rsqrt(spread + epsilon)[None]).reshape(512, 384)
    for part in range(3):
        major[part] = scaled[:, 128 * part:128 * part + 128]
    lane = lax.broadcasted_iota(jnp.int32, (64, 128), 1)
    w = w_ref[...]
    for pair in range(4):
        mids = []
        for i in (2 * pair, 2 * pair + 1):
            mixed = [
                major[part, pl.ds(i, 64, stride=8), :] * scale[:, 128 * part:128 * part + 128]
                + shift[:, 128 * part:128 * part + 128]
                for part in range(3)
            ]
            mids.append(mixed[1])
            ends = jnp.concatenate([mixed[0], mixed[2]], axis=0).astype(bf16)
            wide = lax.dot_general(ends, w, TN, preferred_element_type=f32)
            out_ref[i, 0:128] = (gate_ref[i, 0:128] * wide).astype(bf16)
        top = jnp.where(lane < 64, mids[0], pltpu.roll(mids[1], 64, 1))
        low = jnp.where(lane < 64, pltpu.roll(mids[0], 64, 1), mids[1])
        both = jnp.concatenate([top, low], axis=0).astype(bf16)
        wide = lax.dot_general(both, w, TN, preferred_element_type=f32)
        for n in range(2):
            i = 2 * pair + n
            out_ref[i, 128:192] = (gate_ref[i, 128:192] * wide[64 * n:64 * n + 64]).astype(bf16)


def finish(triangle, gate, gain, bias, w_out):
    whole = lambda shape: pl.BlockSpec(shape, lambda i: (0,) * len(shape))
    return pl.pallas_call(
        finish_kernel,
        name="finish",
        grid=(3,),
        out_shape=jax.ShapeDtypeStruct((24, 192, 128), bf16),
        in_specs=[
            pl.BlockSpec((CHIPS, 1, 8, 384), lambda i: (0, i, 0, 0)),
            pl.BlockSpec((8, 192, 128), lambda i: (i, 0, 0)),
            whole((1, 128)), whole((1, 128)), whole((128, 128)),
        ],
        out_specs=pl.BlockSpec((8, 192, 128), lambda i: (i, 0, 0)),
        scratch_shapes=[
            pltpu.VMEM((64, 384), f32),
            pltpu.VMEM((64, 384), f32),
            pltpu.VMEM((3, 512, 128), f32),
        ],
        compiler_params=pltpu.CompilerParams(dimension_semantics=("arbitrary",)),
    )(triangle, gate, gain, bias, w_out)


def on_device(pair, ln_in_gain, ln_in_bias, w_proj, w_gate, ln_out_gain, ln_out_bias, w_out):
    left, right, gate = project(
        pair, ln_in_gain.reshape(1, 128), ln_in_bias.reshape(1, 128), w_proj, w_gate
    )
    triangle = exchange(left, right)
    return finish(
        triangle, gate, ln_out_gain.reshape(1, 128), ln_out_bias.reshape(1, 128), w_out
    )


def solution(mesh):
    return jax.shard_map(
        on_device,
        mesh=mesh,
        in_specs=(P("row", "loop", None), P(), P(), P(), P(), P(), P(), P()),
        out_specs=P("row", "loop", None),
        check_vma=False,
    )
```

time: 1220 us -> 74.3 us (0.06)
  waiting for transfers between devices: 1140 us -> 0 us
  Pallas kernels: 0 us -> 74.1 us
  matrix products: 26.1 us -> 0 us
  local copies, waits for them, and re-layouts: 18.7 us -> 0 us
  between operations: 13.6 us -> 0.01 us
    all_gather x2 -> x0, waiting for transfers between devices: 1030 us -> none  [the longest x1 990 us: on_device(): lax.all_gather(right_major, 'row', axis=1, tiled=True)]
    all_to_all x1 -> x0, waiting for transfers between devices: 109 us -> none  [on_device(): lax.all_to_all(left_wide, 'row', split_axis=1, concat_axis=0, tiled=True)]
    pallas_call x0 -> x3, Pallas kernels: none -> 74.1 us  [the longest x1 59.6 us: exchange(): pl.pallas_call(exchange_kernel, name='exchange', out_shape=jax.ShapeDtype...]
    dot_general x5 -> x0, matrix products: 26.1 us -> none  [the longest x1 19.3 us: on_device(): lax.dot_general(left_major, lax.all_gather(right_major, 'row', axis=1, ti...]
    all_to_all x2 -> x0, local copies, waits for them, and re-layouts: 13.3 us -> none  [on_device(): lax.all_to_all(left_wide, 'row', split_axis=1, concat_axis=0, tiled=True)]
  transfers between devices with their start and end apart: 3 -> 0, of which waited for: 3 -> 0; matrix products, arithmetic and copies ran while one was open for 2% -> 0% of each run, Pallas kernels for 0% -> 0%
where the time goes in v1:
time: 74.3 us; the launch traced here: 74.1 us
  Pallas kernels  74.1 us (100%)
    pallas_call x1, Pallas kernels, exchange(): pl.pallas_call(exchange_kernel, name='exchange', out_shape=jax.ShapeDtype...  59.6 us
    pallas_call x1, Pallas kernels, project(): pl.pallas_call(project_kernel, name='project', grid=(3,), out_shape=(mess...  9.5 us
    pallas_call x1, Pallas kernels, finish(): pl.pallas_call(finish_kernel, name='finish', grid=(3,), out_shape=jax.Sha...  5.01 us

profile of v1, /device:TPU:0, one launch (start us, length us, event | category | flops | bytes accessed | tf_op | source)
XLA Modules:
  0.0 74.1 jit_solution(3173889672498945235)
XLA Ops:
  0.0 9.5 %project.1 = (bf16[64,3,8,384]{3,2,1,0:T(8,128)(2,1)}, bf16[64,3,8,384]{3,2,1,0:T(8,128)(2,1)}, f32[24,192,128]{2,1,0:T(8,128)}) custom-call(bf16[24,192,128]{2,1,0:T(8,128)(2,1)} %pair_ref.1, f32[1,128]{1,0:T(1,128)} %bitcast.4, f32[1,128]{1,0:T(1,128)} %bitcast.5, bf16[128,512]{1,0:T(8,128)(2,1)} %w_ref.2, bf16[128,128]{1,0:T(8,128)(2,1)} %wg_ref.1), custom_call_target="tpu_custom_call" | custom-call | tf_op jit(solution)/shard_map/project/pallas_call | solution.py:69
  9.5 59.6 %exchange.1.t_ref = bf16[64,3,8,384]{3,2,1,0:T(8,128)(2,1)} custom-call(bf16[64,3,8,384]{3,2,1,0:T(8,128)(2,1)} %get-tuple-element.8.left_ref, bf16[64,3,8,384]{3,2,1,0:T(8,128)(2,1)} %get-tuple-element.9.right_ref), custom_call_target="tpu_custom_call" | custom-call | tf_op jit(solution)/shard_map/exchange/pallas_call | solution.py:207
  69.1 5.0 %finish.1 = bf16[24,192,128]{2,1,0:T(8,128)(2,1)} custom-call(bf16[64,3,8,384]{3,2,1,0:T(8,128)(2,1)} %exchange.1.t_ref, f32[24,192,128]{2,1,0:T(8,128)} %get-tuple-element.10.gate_ref, f32[1,128]{1,0:T(1,128)} %bitcast.6, f32[1,128]{1,0:T(1,128)} %bitcast.7, bf16[128,128]{1,0:T(8,128)(2,1)} %w_ref.3), custom_call_target="tpu_custom_call" | custom-call | tf_op jit(solution)/shard_map/finish/pallas_call | solution.py:276

commit v2 on v0

v2 whole, which is shorter than its diff:
```python
import jax
import jax.numpy as jnp
from jax import lax
from jax.experimental import pallas as pl
from jax.experimental.pallas import tpu as pltpu
from jax.sharding import PartitionSpec as P

epsilon = 1e-05
MESH = pl.DeviceIdType.MESH
f32 = jnp.float32
bf16 = jnp.bfloat16
CHIPS = 64
NT = (((1,), (1,)), ((), ()))
TN = (((0,), (0,)), ((), ()))


def normalize(values, gain, bias):
    center = values - jnp.mean(values, axis=-1, keepdims=True)
    spread = jnp.mean(center * center, axis=-1, keepdims=True)
    return center * lax.rsqrt(spread + epsilon) * gain + bias


def over_channels(values):
    total = jnp.sum(values, axis=0)
    ends = total[:, 0:128] + total[:, 256:384]
    mid = total[:, 128:256]
    mid = mid + pltpu.roll(mid, 64, 1)
    return jnp.concatenate([ends, mid, ends], axis=1) * (1.0 / 128)


def kernel(pair_ref, gain_ref, bias_ref, w_ref, wg_ref, out_gain_ref, out_bias_ref, wo_ref, out_ref,
           wide, tall, normed, gate, major, message, own, other, acc, mid0, out0, out1, got0, got1,
           scale, shift, mixing,
           send_m, recv_m, pass_send, pass_recv, send_t0, recv_t0, send_t1, recv_t1):
    row = lax.axis_index("row")
    loop = lax.axis_index("loop")
    core = loop % 2
    y_hi = loop // 2
    x = row // 8
    z = (row // 2) % 4
    y = y_hi * 2 + row % 2
    me = y_hi * 32 + row
    twin = (row, y_hi * 2 + (1 - core))

    def target(n):
        o = (n * 21) % CHIPS
        tx = (x + o // 16) % 4
        ty = (y + (o // 4) % 4) % 4
        tz = (z + o % 4) % 4
        t_row = (tx * 4 + tz) * 2 + ty % 2
        return (ty // 2) * 32 + t_row, (t_row, (ty // 2) * 2 + core)

    barrier = pltpu.get_barrier_semaphore()

    def greet(n, carry):
        _, device = target(n)
        pl.semaphore_signal(barrier, inc=1, device_id=device, device_id_type=MESH)
        return carry

    lax.fori_loop(1, CHIPS, greet, 0)
    pl.semaphore_signal(barrier, inc=1, device_id=twin, device_id_type=MESH)

    flipped = w_ref[...].astype(f32).T.astype(bf16)
    for g in range(2):
        for kind in range(4):
            part = flipped[128 * kind + 64 * g:128 * kind + 64 * g + 64]
            wide[g, pl.ds(64 * kind, 64)] = part
            tall[g, pl.ds(64 * (kind % 2), 64), pl.ds(128 * (kind // 2), 128)] = part

    def project(g, kc):
        for k in range(8):
            values = normed[8 * kc + k]
            head = values[0:128]
            rest = values[128:192]
            zero = jnp.zeros_like(rest)
            both = jnp.concatenate(
                [jnp.concatenate([rest, zero], axis=1), jnp.concatenate([zero, rest], axis=1)],
                axis=0,
            )
            a = lax.dot_general(wide[g], head, NT, preferred_element_type=f32)
            b = lax.dot_general(tall[g], both, NT, preferred_element_type=f32)
            rows = pl.ds(64 * k, 64)
            major[0, rows] = jax.nn.sigmoid(a[0:64]) * a[64:128]
            major[1, rows] = jax.nn.sigmoid(b[0:64]) * b[64:128]
            major[2, rows] = jax.nn.sigmoid(a[128:192]) * a[192:256]
        for c in range(CHIPS):
            for part in range(3):
                message[g, c, kc, :, pl.ds(128 * part, 128)] = (
                    major[part, pl.ds(c, 8, stride=64), :].astype(bf16)
                )

    def send_chunk(g, kc):
        def body(n, carry):
            chip, device = target(n)
            pltpu.make_async_remote_copy(
                message.at[g, chip, kc], own.at[g, me, kc], send_m.at[g], recv_m.at[g, kc],
                device_id=device, device_id_type=MESH,
            ).start()
            return carry

        lax.fori_loop(1, CHIPS, body, 0)
        pltpu.make_async_copy(message.at[g, me, kc], own.at[g, me, kc], recv_m.at[g, kc]).start()

    def first(kc):
        for k in range(8):
            values = pair_ref[8 * kc + k].astype(f32)
            normed[8 * kc + k] = normalize(values, gain_ref[...], bias_ref[...]).astype(bf16)
        project(0, kc)

    first(0)
    pl.semaphore_wait(barrier, CHIPS)
    send_chunk(0, 0)

    def rest_of_first(kc, carry):
        first(kc)
        send_chunk(0, kc)
        return carry

    lax.fori_loop(1, 3, rest_of_first, 0)

    def second(kc, carry):
        project(1, kc)
        send_chunk(1, kc)
        return carry

    lax.fori_loop(0, 3, second, 0)

    def open_gate(k, carry):
        gate[k] = jax.nn.sigmoid(jnp.dot(normed[k], wg_ref[...], preferred_element_type=f32))
        return carry

    lax.fori_loop(0, 24, open_gate, 0)

    diagonal = (lax.broadcasted_iota(jnp.int32, (128, 128), 0)
                == lax.broadcasted_iota(jnp.int32, (128, 128), 1))
    lane64 = lax.broadcasted_iota(jnp.int32, (64, 128), 1)
    lane192 = lax.broadcasted_iota(jnp.int32, (192, 128), 1)
    for source, dest in ((out_gain_ref, scale), (out_bias_ref, shift)):
        column = jnp.sum(jnp.where(diagonal, source[...], 0.0), axis=1, keepdims=True)
        spread_out = jnp.broadcast_to(column, (128, 128))
        dest[0] = spread_out[0:64]
        dest[1] = jnp.where(lane64 < 64, spread_out[0:64], spread_out[64:128])
        dest[2] = spread_out[64:128]

    def multiply(g, kc, left_ref, of):
        def block(h, carry):
            left = left_ref[g, pl.ds(h * 32, 32), kc, :, 0:256].reshape(256, 256).T[0:192]
            for j in range(2):
                right = own[g, 32 * j:32 * j + 32, kc, :, 128:384].reshape(256, 256)
                acc[h * 2 + of, j] += jnp.dot(left, right, preferred_element_type=f32)
            return carry

        lax.fori_loop(0, 2, block, 0)

    def gather(g):
        acc[...] = jnp.zeros_like(acc)

        def chunk(kc, carry):
            pltpu.make_async_copy(own.at[g, :, kc], own.at[g, :, kc], recv_m.at[g, kc]).wait()
            passing = pltpu.make_async_remote_copy(
                own.at[g, :, kc, :, pl.ds(0, 256)], other.at[g, :, kc],
                pass_send.at[g, kc], pass_recv.at[g, kc], device_id=twin, device_id_type=MESH,
            )
            passing.start()
            multiply(g, kc, own, core)
            passing.wait()
            multiply(g, kc, other, 1 - core)
            return carry

        lax.fori_loop(0, 3, chunk, 0)

    gather(0)

    def close_first(n, carry):
        block = n % 4
        j = n // 4
        t = acc[block, j]
        out0[pl.ds(j * 32 + block * 8, 8)] = t[:, 128:256].reshape(8, 3, 8, 128).astype(bf16)
        mid0[block, j] = pltpu.roll(t[:, 0:128], 64, 1)
        return carry

    lax.fori_loop(0, 8, close_first, 0)

    def ship_first(n, carry):
        chip, device = target(n)
        pltpu.make_async_remote_copy(
            out0.at[chip], got0.at[me], send_t0, recv_t0, device_id=device, device_id_type=MESH
        ).start()
        return carry

    lax.fori_loop(1, CHIPS, ship_first, 0)
    pltpu.make_async_copy(out0.at[me], got0.at[me], recv_t0).start()

    gather(1)

    def close_second(n, carry):
        block = n % 4
        j = n // 4
        t = acc[block, j]
        mid = jnp.where(lane192 < 64, mid0[block, j], t[:, 0:128])
        t = jnp.concatenate([mid, t[:, 128:256]], axis=1)
        out1[pl.ds(j * 32 + block * 8, 8)] = t.reshape(8, 3, 8, 256).astype(bf16)
        return carry

    lax.fori_loop(0, 8, close_second, 0)

    def ship_second(it, carry):
        def body(n, inner):
            chip, device = target(n)
            pltpu.make_async_remote_copy(
                out1.at[chip, it], got1.at[me, it], send_t1, recv_t1.at[it],
                device_id=device, device_id_type=MESH,
            ).start()
            return inner

        lax.fori_loop(1, CHIPS, body, 0)
        pltpu.make_async_copy(out1.at[me, it], got1.at[me, it], recv_t1.at[it]).start()
        return carry

    lax.fori_loop(0, 3, ship_second, 0)

    pltpu.make_async_copy(out0, got0, recv_t0).wait()

    def finish(it, carry):
        pltpu.make_async_copy(out1.at[:, it], got1.at[:, it], recv_t1.at[it]).wait()
        t = jnp.concatenate([got0[:, it], got1[:, it]], axis=-1).astype(f32)
        center = t - over_channels(t)[None]
        spread = over_channels(center * center)
        scaled = (center * lax.rsqrt(spread + epsilon)[None]).reshape(512, 384)
        for part in range(3):
            mixing[part] = scaled[:, 128 * part:128 * part + 128]
        w = wo_ref[...]
        for pair in range(4):
            mids = []
            for n in range(2):
                i = 2 * pair + n
                mixed = [
                    mixing[part, pl.ds(i, 64, stride=8), :] * scale[part] + shift[part]
                    for part in range(3)
                ]
                mids.append(mixed[1])
                ends = jnp.concatenate([mixed[0], mixed[2]], axis=0).astype(bf16)
                result = lax.dot_general(ends, w, TN, preferred_element_type=f32)
                k = 8 * it + i
                out_ref[k, 0:128] = (gate[k, 0:128] * result).astype(bf16)
            top = jnp.where(lane64 < 64, mids[0], pltpu.roll(mids[1], 64, 1))
            low = jnp.where(lane64 < 64, pltpu.roll(mids[0], 64, 1), mids[1])
            both = jnp.concatenate([top, low], axis=0).astype(bf16)
            result = lax.dot_general(both, w, TN, preferred_element_type=f32)
            for n in range(2):
                k = 8 * it + 2 * pair + n
                out_ref[k, 128:192] = (gate[k, 128:192] * result[64 * n:64 * n + 64]).astype(bf16)
        return carry

    lax.fori_loop(0, 3, finish, 0)

    most = pl.ds(0, CHIPS - 1)
    for g in range(2):
        pltpu.make_async_copy(message.at[g, most], own.at[g, most], send_m.at[g]).wait()
    pltpu.make_async_copy(out0.at[most], got0.at[most], send_t0).wait()
    pltpu.make_async_copy(out1.at[most], got1.at[most], send_t1).wait()


def on_device(pair, ln_in_gain, ln_in_bias, w_proj, w_gate, ln_out_gain, ln_out_bias, w_out):
    dma = pltpu.SemaphoreType.DMA
    vmem = pl.BlockSpec(memory_space=pltpu.VMEM)
    return pl.pallas_call(
        kernel,
        name="triangle",
        out_shape=jax.ShapeDtypeStruct((24, 192, 128), bf16),
        in_specs=[vmem] * 8,
        out_specs=vmem,
        scratch_shapes=[
            pltpu.VMEM((2, 256, 128), bf16),
            pltpu.VMEM((2, 128, 256), bf16),
            pltpu.VMEM((24, 192, 128), bf16),
            pltpu.VMEM((24, 192, 128), f32),
            pltpu.VMEM((3, 512, 128), f32),
            pltpu.VMEM((2, CHIPS, 3, 8, 384), bf16),
            pltpu.VMEM((2, CHIPS, 3, 8, 384), bf16),
            pltpu.VMEM((2, CHIPS, 3, 8, 256), bf16),
            pltpu.VMEM((4, 2, 192, 256), f32),
            pltpu.VMEM((4, 2, 192, 128), f32),
            pltpu.VMEM((CHIPS, 3, 8, 128), bf16),
            pltpu.VMEM((CHIPS, 3, 8, 256), bf16),
            pltpu.VMEM((CHIPS, 3, 8, 128), bf16),
            pltpu.VMEM((CHIPS, 3, 8, 256), bf16),
            pltpu.VMEM((3, 64, 128), f32),
            pltpu.VMEM((3, 64, 128), f32),
            pltpu.VMEM((3, 512, 128), f32),
            dma((2,)), dma((2, 3)), dma((2, 3)), dma((2, 3)), dma, dma, dma, dma((3,)),
        ],
        compiler_params=pltpu.CompilerParams(collective_id=0, has_side_effects=True),
    )(pair, ln_in_gain.reshape(1, 128), ln_in_bias.reshape(1, 128), w_proj, w_gate,
      ln_out_gain.reshape(1, 128), ln_out_bias.reshape(1, 128), w_out)


def solution(mesh):
    return jax.shard_map(
        on_device,
        mesh=mesh,
        in_specs=(P("row", "loop", None), P(), P(), P(), P(), P(), P(), P()),
        out_specs=P("row", "loop", None),
        check_vma=False,
    )
```

time: 1220 us -> 69.2 us (0.06)
  waiting for transfers between devices: 1140 us -> 0 us
  Pallas kernels: 0 us -> 66.1 us
  matrix products: 26.1 us -> 0 us
  local copies, waits for them, and re-layouts: 18.7 us -> 2.36 us
  between operations: 13.6 us -> 0.01 us
    all_gather x2 -> x0, waiting for transfers between devices: 1030 us -> none  [the longest x1 990 us: on_device(): lax.all_gather(right_major, 'row', axis=1, tiled=True)]
    all_to_all x1 -> x0, waiting for transfers between devices: 109 us -> none  [on_device(): lax.all_to_all(left_wide, 'row', split_axis=1, concat_axis=0, tiled=True)]
    pallas_call x0 -> x1, Pallas kernels: none -> 66.1 us  [on_device(): pl.pallas_call(kernel, name='triangle', out_shape=jax.ShapeDtypeStruct((2...]
    dot_general x5 -> x0, matrix products: 26.1 us -> none  [the longest x1 19.3 us: on_device(): lax.dot_general(left_major, lax.all_gather(right_major, 'row', axis=1, ti...]
    all_to_all x2 -> x0, local copies, waits for them, and re-layouts: 13.3 us -> none  [on_device(): lax.all_to_all(left_wide, 'row', split_axis=1, concat_axis=0, tiled=True)]
  transfers between devices with their start and end apart: 3 -> 0, of which waited for: 3 -> 0; matrix products, arithmetic and copies ran while one was open for 2% -> 0% of each run, Pallas kernels for 0% -> 0%
where the time goes in v2:
time: 69.2 us; the launch traced here: 68.4 us
  Pallas kernels  66.1 us (96%)
  local copies, waits for them, and re-layouts  2.36 us (3%)
    pallas_call x1, Pallas kernels, on_device(): pl.pallas_call(kernel, name='triangle', out_shape=jax.ShapeDtypeStruct((2...  66.1 us
    unnamed x1, local copies, waits for them, and re-layouts  2.36 us

profile of v2, /device:TPU:0, one launch (start us, length us, event | category | flops | bytes accessed | tf_op | source)
XLA Modules:
  0.0 68.4 jit_solution(15804348407352340240)
XLA Ops:
  0.0 66.1 %triangle.1 = bf16[24,192,128]{2,1,0:T(8,128)(2,1)} custom-call(bf16[24,192,128]{2,1,0:T(8,128)(2,1)} %pair_ref.1, f32[1,128]{1,0:T(1,128)} %bitcast.4, f32[1,128]{1,0:T(1,128)} %bitcast.5, bf16[128,512]{1,0:T(8,128)(2,1)} %w_ref.1, bf16[128,128]{1,0:T(8,128)(2,1)} %wg_ref.1, f32[1,128]{1,0:T(1,128)} %bitcast.6, f32[1,128]{1,0:T(1,128)} %bitcast.7, ...), custom_call_target="tpu_custom_call" | custom-call | tf_op jit(solution)/shard_map/triangle/pallas_call | solution.py:267
  66.1 2.4 %copy.10 = bf16[24,192,128]{2,1,0:T(8,128)(2,1)} copy(bf16[24,192,128]{2,1,0:T(8,128)(2,1)} %triangle.1) | data formatting | bytes 2359296

commit v3 on v2

v3 whole, which is shorter than its diff:
```python
import jax
import jax.numpy as jnp
from jax import lax
from jax.experimental import pallas as pl
from jax.experimental.pallas import tpu as pltpu
from jax.sharding import PartitionSpec as P

epsilon = 1e-05
MESH = pl.DeviceIdType.MESH
f32 = jnp.float32
bf16 = jnp.bfloat16
CHIPS = 64
NT = (((1,), (1,)), ((), ()))
TN = (((0,), (0,)), ((), ()))


def distance(o):
    return sum(min(d, 4 - d) for d in (o // 16, o // 4 % 4, o % 4))


FAR_FIRST = sorted(range(1, CHIPS), key=lambda o: (-distance(o), o * 21 % CHIPS))


def normalize(values, gain, bias):
    center = values - jnp.mean(values, axis=-1, keepdims=True)
    spread = jnp.mean(center * center, axis=-1, keepdims=True)
    return center * lax.rsqrt(spread + epsilon) * gain + bias


def over_channels(ends, mid):
    ends = jnp.sum(ends, axis=0)
    mid = jnp.sum(mid, axis=0)
    return ends * (1.0 / 128), (mid + pltpu.roll(mid, 64, 1)) * (1.0 / 128)


def kernel(pair_ref, gain_ref, bias_ref, w_ref, wg_ref, out_gain_ref, out_bias_ref, wo_ref, out_ref,
           wide, tall, normed, gate, major, sent_l, sent_r, own, other, right, turned, sent_t, got_t,
           scale, shift, mixing,
           send_l, recv_l, pass_send, pass_recv, send_r, recv_r, send_t, recv_t, recv_last):
    row = lax.axis_index("row")
    loop = lax.axis_index("loop")
    core = loop % 2
    y_hi = loop // 2
    x = row // 8
    z = (row // 2) % 4
    y = y_hi * 2 + row % 2
    me = y_hi * 32 + row
    twin = (row, y_hi * 2 + (1 - core))
    xs = [((x + d) % 4) * 8 for d in range(4)]
    zs = [((z + d) % 4) * 2 for d in range(4)]
    ys = [(y + d) % 4 for d in range(4)]
    y_his = [v // 2 for v in ys]
    y_los = [v % 2 for v in ys]

    def each_peer(act):
        for o in FAR_FIRST:
            dy = o // 4 % 4
            t_row = xs[o // 16] + zs[o % 4] + y_los[dy]
            act(y_his[dy] * 32 + t_row, (t_row, y_his[dy] * 2 + core))

    def send(src, dst, send_sem, recv_sem):
        def act(chip, device):
            pltpu.make_async_remote_copy(
                src(chip), dst, send_sem, recv_sem, device_id=device, device_id_type=MESH
            ).start()

        each_peer(act)
        pltpu.make_async_copy(src(me), dst, recv_sem).start()

    barrier = pltpu.get_barrier_semaphore()
    each_peer(lambda chip, device: pl.semaphore_signal(
        barrier, inc=1, device_id=device, device_id_type=MESH))
    pl.semaphore_signal(barrier, inc=1, device_id=twin, device_id_type=MESH)

    flipped = w_ref[...].astype(f32).T.astype(bf16)
    for side in range(2):
        wide[side] = flipped[256 * side:256 * side + 256]
        for kind in range(2):
            for half in range(2):
                at = 256 * side + 128 * kind + 64 * half
                tall[side, pl.ds(64 * kind, 64), pl.ds(128 * half, 128)] = flipped[at:at + 64]

    def project(side, kc):
        for k in range(8):
            values = normed[8 * kc + k]
            head = values[0:128]
            rest = values[128:192]
            zero = jnp.zeros_like(rest)
            both = jnp.concatenate(
                [jnp.concatenate([rest, zero], axis=1), jnp.concatenate([zero, rest], axis=1)],
                axis=0,
            )
            a = lax.dot_general(wide[side], head, NT, preferred_element_type=f32)
            b = lax.dot_general(tall[side], both, NT, preferred_element_type=f32)
            rows = pl.ds(64 * k, 64)
            ends = jax.nn.sigmoid(a[0:128]) * a[128:256]
            major[0, rows] = ends[0:64]
            major[1, rows] = jax.nn.sigmoid(b[0:64]) * b[64:128]
            major[2, rows] = ends[64:128]

    def column(part, c):
        return major[part, pl.ds(c, 8, stride=64), :].astype(bf16)

    def project_left(kc):
        for k in range(8):
            values = pair_ref[8 * kc + k].astype(f32)
            normed[8 * kc + k] = normalize(values, gain_ref[...], bias_ref[...]).astype(bf16)
        project(0, kc)
        for c in range(CHIPS):
            for part in range(3):
                sent_l[c, kc, :, pl.ds(128 * part, 128)] = column(part, c)

    def send_left(kc):
        send(lambda chip: sent_l.at[chip, kc], own.at[me, kc], send_l, recv_l.at[kc])

    project_left(0)
    pl.semaphore_wait(barrier, CHIPS)
    send_left(0)

    def rest_of_left(kc, carry):
        project_left(kc)
        send_left(kc)
        return carry

    lax.fori_loop(1, 3, rest_of_left, 0)

    def project_right(kc, carry):
        project(1, kc)
        for c in range(CHIPS):
            for part in range(3):
                sent_r[part, c, kc] = column(part, c)
        return carry

    lax.fori_loop(0, 3, project_right, 0)

    def send_right(part, carry):
        send(lambda chip: sent_r.at[part, chip], right.at[part, me], send_r.at[part],
             recv_r.at[part])
        return carry

    lax.fori_loop(0, 3, send_right, 0)

    def open_gate(k, carry):
        gate[k] = jax.nn.sigmoid(jnp.dot(normed[k], wg_ref[...], preferred_element_type=f32))
        return carry

    lax.fori_loop(0, 24, open_gate, 0)

    diagonal = (lax.broadcasted_iota(jnp.int32, (128, 128), 0)
                == lax.broadcasted_iota(jnp.int32, (128, 128), 1))
    lane64 = lax.broadcasted_iota(jnp.int32, (64, 128), 1)
    for source, dest in ((out_gain_ref, scale), (out_bias_ref, shift)):
        one = jnp.sum(jnp.where(diagonal, source[...], 0.0), axis=1, keepdims=True)
        spread_out = jnp.broadcast_to(one, (128, 128))
        dest[0] = spread_out[0:64]
        dest[1] = jnp.where(lane64 < 64, spread_out[0:64], spread_out[64:128])
        dest[2] = spread_out[64:128]

    def turn(ref, kc, of):
        def block(h, carry):
            t = ref[pl.ds(h * 32, 32), kc].reshape(256, 384).T
            first = (h * 2 + of) * 192
            lanes = pl.ds(pl.multiple_of(kc * 256, 256), 256)
            turned[0, pl.ds(pl.multiple_of(first, 64), 192), lanes] = t[0:192]
            turned[1, pl.ds(pl.multiple_of(first + 128, 64), 64), lanes] = t[192:256]
            turned[1, pl.ds(pl.multiple_of(first, 64), 128), lanes] = t[256:384]
            return carry

        lax.fori_loop(0, 2, block, 0)

    def take_left(kc, carry):
        pltpu.make_async_copy(own.at[:, kc], own.at[:, kc], recv_l.at[kc]).wait()
        passing = pltpu.make_async_remote_copy(
            own.at[:, kc], other.at[:, kc], pass_send.at[kc], pass_recv.at[kc],
            device_id=twin, device_id_type=MESH,
        )
        passing.start()
        turn(own, kc, core)
        passing.wait()
        turn(other, kc, 1 - core)
        return carry

    lax.fori_loop(0, 3, take_left, 0)

    def factor(part):
        pltpu.make_async_copy(sent_r.at[part], right.at[part], recv_r.at[part]).wait()
        return [
            jnp.concatenate(
                [right[part, 32 * j:32 * j + 32, kc].reshape(256, 128) for j in range(2)], axis=1
            )
            for kc in range(3)
        ]

    def multiply(channel, factors):
        return sum(
            jnp.dot(turned[channel, :, 256 * kc:256 * kc + 256], factors[kc],
                    preferred_element_type=f32)
            for kc in range(3)
        )

    def keep(part, j, t):
        sent_t[part, 32 * j:32 * j + 32] = t.reshape(32, 3, 8, 128).astype(bf16)

    def send_part(part):
        send(lambda chip: sent_t.at[part, chip], got_t.at[part, me], send_t.at[part],
             recv_t.at[part])

    factors = factor(0)
    t = multiply(0, factors)
    for j in range(2):
        keep(0, j, t[:, 128 * j:128 * j + 128])
    send_part(0)

    factors = factor(1)
    t0 = multiply(0, factors)
    t1 = multiply(1, factors)
    lane768 = lax.broadcasted_iota(jnp.int32, (768, 128), 1)
    for j in range(2):
        lanes = slice(128 * j, 128 * j + 128)
        keep(1, j, jnp.where(lane768 < 64, t0[:, lanes], t1[:, lanes]))
    send_part(1)

    factors = factor(2)
    t = multiply(1, factors)
    for j in range(2):
        keep(2, j, t[:, 128 * j:128 * j + 128])

    def send_last(it, carry):
        send(lambda chip: sent_t.at[2, chip, it], got_t.at[2, me, it], send_t.at[2],
             recv_last.at[it])
        return carry

    lax.fori_loop(0, 3, send_last, 0)

    for part in range(2):
        pltpu.make_async_copy(sent_t.at[part], got_t.at[part], recv_t.at[part]).wait()

    def finish(it, carry):
        pltpu.make_async_copy(sent_t.at[2, :, it], got_t.at[2, :, it], recv_last.at[it]).wait()
        t0, mid, t2 = [got_t[part, :, it].astype(f32) for part in range(3)]
        ends_mean, mid_mean = over_channels(t0 + t2, mid)
        t0 = t0 - ends_mean[None]
        t2 = t2 - ends_mean[None]
        mid = mid - mid_mean[None]
        ends_spread, mid_spread = over_channels(t0 * t0 + t2 * t2, mid * mid)
        ends_root = lax.rsqrt(ends_spread + epsilon)[None]
        mid_root = lax.rsqrt(mid_spread + epsilon)[None]
        mixing[0] = (t0 * ends_root).reshape(512, 128)
        mixing[1] = (mid * mid_root).reshape(512, 128)
        mixing[2] = (t2 * ends_root).reshape(512, 128)
        w = wo_ref[...]
        for pair in range(4):
            mids = []
            for n in range(2):
                i = 2 * pair + n
                mixed = [
                    mixing[part, pl.ds(i, 64, stride=8), :] * scale[part] + shift[part]
                    for part in range(3)
                ]
                mids.append(mixed[1])
                ends = jnp.concatenate([mixed[0], mixed[2]], axis=0).astype(bf16)
                result = lax.dot_general(ends, w, TN, preferred_element_type=f32)
                k = 8 * it + i
                out_ref[k, 0:128] = (gate[k, 0:128] * result).astype(bf16)
            top = jnp.where(lane64 < 64, mids[0], pltpu.roll(mids[1], 64, 1))
            low = jnp.where(lane64 < 64, pltpu.roll(mids[0], 64, 1), mids[1])
            both = jnp.concatenate([top, low], axis=0).astype(bf16)
            result = lax.dot_general(both, w, TN, preferred_element_type=f32)
            for n in range(2):
                k = 8 * it + 2 * pair + n
                out_ref[k, 128:192] = (gate[k, 128:192] * result[64 * n:64 * n + 64]).astype(bf16)
        return carry

    lax.fori_loop(0, 3, finish, 0)

    most = pl.ds(0, CHIPS - 1)
    pltpu.make_async_copy(sent_l.at[most], own.at[most], send_l).wait()
    for part in range(3):
        pltpu.make_async_copy(sent_r.at[part, most], right.at[part, most], send_r.at[part]).wait()
        pltpu.make_async_copy(sent_t.at[part, most], got_t.at[part, most], send_t.at[part]).wait()


def on_device(pair, ln_in_gain, ln_in_bias, w_proj, w_gate, ln_out_gain, ln_out_bias, w_out):
    dma = pltpu.SemaphoreType.DMA
    vmem = pl.BlockSpec(memory_space=pltpu.VMEM)
    return pl.pallas_call(
        kernel,
        name="triangle",
        out_shape=jax.ShapeDtypeStruct((24, 192, 128), bf16),
        in_specs=[vmem] * 8,
        out_specs=vmem,
        scratch_shapes=[
            pltpu.VMEM((2, 256, 128), bf16),
            pltpu.VMEM((2, 128, 256), bf16),
            pltpu.VMEM((24, 192, 128), bf16),
            pltpu.VMEM((24, 192, 128), f32),
            pltpu.VMEM((3, 512, 128), f32),
            pltpu.VMEM((CHIPS, 3, 8, 384), bf16),
            pltpu.VMEM((3, CHIPS, 3, 8, 128), bf16),
            pltpu.VMEM((CHIPS, 3, 8, 384), bf16),
            pltpu.VMEM((CHIPS, 3, 8, 384), bf16),
            pltpu.VMEM((3, CHIPS, 3, 8, 128), bf16),
            pltpu.VMEM((2, 768, 768), bf16),
            pltpu.VMEM((3, CHIPS, 3, 8, 128), bf16),
            pltpu.VMEM((3, CHIPS, 3, 8, 128), bf16),
            pltpu.VMEM((3, 64, 128), f32),
            pltpu.VMEM((3, 64, 128), f32),
            pltpu.VMEM((3, 512, 128), f32),
            dma, dma((3,)), dma((3,)), dma((3,)), dma((3,)), dma((3,)), dma((3,)), dma((3,)), dma((3,)),
        ],
        compiler_params=pltpu.CompilerParams(collective_id=0, has_side_effects=True),
    )(pair, ln_in_gain.reshape(1, 128), ln_in_bias.reshape(1, 128), w_proj, w_gate,
      ln_out_gain.reshape(1, 128), ln_out_bias.reshape(1, 128), w_out)


def solution(mesh):
    return jax.shard_map(
        on_device,
        mesh=mesh,
        in_specs=(P("row", "loop", None), P(), P(), P(), P(), P(), P(), P()),
        out_specs=P("row", "loop", None),
        check_vma=False,
    )
```

time: 69.2 us -> 56 us (0.81)
  Pallas kernels: 66.1 us -> 53.4 us
    pallas_call x1, Pallas kernels: 66.1 us -> 53.4 us  [on_device(): pl.pallas_call(kernel, name='triangle', out_shape=jax.ShapeDtypeStruct((2...]
where the time goes in v3:
time: 56 us; the launch traced here: 55.8 us
  Pallas kernels  53.4 us (95%)
  local copies, waits for them, and re-layouts  2.36 us (4%)
    pallas_call x1, Pallas kernels, on_device(): pl.pallas_call(kernel, name='triangle', out_shape=jax.ShapeDtypeStruct((2...  53.4 us
    unnamed x1, local copies, waits for them, and re-layouts  2.36 us

profile of v3, /device:TPU:0, one launch (start us, length us, event | category | flops | bytes accessed | tf_op | source)
XLA Modules:
  0.0 55.8 jit_solution(2039571478944207119)
XLA Ops:
  0.0 53.4 %triangle.1 = bf16[24,192,128]{2,1,0:T(8,128)(2,1)} custom-call(bf16[24,192,128]{2,1,0:T(8,128)(2,1)} %pair_ref.1, f32[1,128]{1,0:T(1,128)} %bitcast.4, f32[1,128]{1,0:T(1,128)} %bitcast.5, bf16[128,512]{1,0:T(8,128)(2,1)} %w_ref.1, bf16[128,128]{1,0:T(8,128)(2,1)} %wg_ref.1, f32[1,128]{1,0:T(1,128)} %bitcast.6, f32[1,128]{1,0:T(1,128)} %bitcast.7, ...), custom_call_target="tpu_custom_call" | custom-call | tf_op jit(solution)/shard_map/triangle/pallas_call | solution.py:286
  53.4 2.4 %copy.10 = bf16[24,192,128]{2,1,0:T(8,128)(2,1)} copy(bf16[24,192,128]{2,1,0:T(8,128)(2,1)} %triangle.1) | data formatting | bytes 2359296

commit v4 on v3

--- a/solution.py
+++ b/solution.py
@@ -33,10 +33,28 @@
     return ends * (1.0 / 128), (mid + pltpu.roll(mid, 64, 1)) * (1.0 / 128)
 
 
-def kernel(pair_ref, gain_ref, bias_ref, w_ref, wg_ref, out_gain_ref, out_bias_ref, wo_ref, out_ref,
+def kernel(pair_hbm, gain_hbm, bias_hbm, w_hbm, wg_hbm, out_gain_hbm, out_bias_hbm, wo_hbm, out_ref,
+           pair_ref, gain_ref, bias_ref, w_ref, wg_ref, out_gain_ref, out_bias_ref, wo_ref,
            wide, tall, normed, gate, major, sent_l, sent_r, own, other, right, turned, sent_t, got_t,
            scale, shift, mixing,
-           send_l, recv_l, pass_send, pass_recv, send_r, recv_r, send_t, recv_t, recv_last):
+           load, load_pair, send_l, recv_l, pass_send, pass_recv, send_r, recv_r, send_t, recv_t, recv_last):
+    def rows_of(kc):
+        rows = pl.ds(pl.multiple_of(kc * 8, 8), 8)
+        return pltpu.make_async_copy(pair_hbm.at[rows], pair_ref.at[rows], load_pair.at[kc])
+
+    loads = [
+        pltpu.make_async_copy(src, dst, load.at[n])
+        for n, (src, dst) in enumerate((
+            (w_hbm, w_ref), (gain_hbm, gain_ref), (bias_hbm, bias_ref), (wg_hbm, wg_ref),
+            (out_gain_hbm, out_gain_ref), (out_bias_hbm, out_bias_ref), (wo_hbm, wo_ref),
+        ))
+    ]
+    loads[0].start()
+    for kc in range(3):
+        rows_of(kc).start()
+    for copy in loads[1:]:
+        copy.start()
+
     row = lax.axis_index("row")
     loop = lax.axis_index("loop")
     core = loop % 2
@@ -72,13 +90,17 @@
         barrier, inc=1, device_id=device, device_id_type=MESH))
     pl.semaphore_signal(barrier, inc=1, device_id=twin, device_id_type=MESH)
 
-    flipped = w_ref[...].astype(f32).T.astype(bf16)
-    for side in range(2):
-        wide[side] = flipped[256 * side:256 * side + 256]
+    def flip(side):
+        flipped = w_ref[:, 256 * side:256 * side + 256].astype(f32).T.astype(bf16)
+        wide[side] = flipped
         for kind in range(2):
             for half in range(2):
-                at = 256 * side + 128 * kind + 64 * half
+                at = 128 * kind + 64 * half
                 tall[side, pl.ds(64 * kind, 64), pl.ds(128 * half, 128)] = flipped[at:at + 64]
+
+    for copy in loads[0:3]:
+        copy.wait()
+    flip(0)
 
     def project(side, kc):
         for k in range(8):
@@ -102,6 +124,7 @@
         return major[part, pl.ds(c, 8, stride=64), :].astype(bf16)
 
     def project_left(kc):
+        rows_of(kc).wait()
         for k in range(8):
             values = pair_ref[8 * kc + k].astype(f32)
             normed[8 * kc + k] = normalize(values, gain_ref[...], bias_ref[...]).astype(bf16)
@@ -124,6 +147,8 @@
 
     lax.fori_loop(1, 3, rest_of_left, 0)
 
+    flip(1)
+
     def project_right(kc, carry):
         project(1, kc)
         for c in range(CHIPS):
@@ -139,6 +164,9 @@
         return carry
 
     lax.fori_loop(0, 3, send_right, 0)
+
+    for copy in loads[3:]:
+        copy.wait()
 
     def open_gate(k, carry):
         gate[k] = jax.nn.sigmoid(jnp.dot(normed[k], wg_ref[...], preferred_element_type=f32))
@@ -286,10 +314,18 @@
     return pl.pallas_call(
         kernel,
         name="triangle",
-        out_shape=jax.ShapeDtypeStruct((24, 192, 128), bf16),
-        in_specs=[vmem] * 8,
+        out_shape=pltpu.VMEM((24, 192, 128), bf16),
+        in_specs=[pl.BlockSpec(memory_space=pl.ANY)] * 8,
         out_specs=vmem,
         scratch_shapes=[
+            pltpu.VMEM((24, 192, 128), bf16),
+            pltpu.VMEM((1, 128), f32),
+            pltpu.VMEM((1, 128), f32),
+            pltpu.VMEM((128, 512), bf16),
+            pltpu.VMEM((128, 128), bf16),
+            pltpu.VMEM((1, 128), f32),
+            pltpu.VMEM((1, 128), f32),
+            pltpu.VMEM((128, 128), bf16),
             pltpu.VMEM((2, 256, 128), bf16),
             pltpu.VMEM((2, 128, 256), bf16),
             pltpu.VMEM((24, 192, 128), bf16),
@@ -306,7 +342,7 @@
             pltpu.VMEM((3, 64, 128), f32),
             pltpu.VMEM((3, 64, 128), f32),
             pltpu.VMEM((3, 512, 128), f32),
-            dma, dma((3,)), dma((3,)), dma((3,)), dma((3,)), dma((3,)), dma((3,)), dma((3,)), dma((3,)),
+            dma((7,)), dma((3,)), dma, dma((3,)), dma((3,)), dma((3,)), dma((3,)), dma((3,)), dma((3,)), dma((3,)), dma((3,)),
         ],
         compiler_params=pltpu.CompilerParams(collective_id=0, has_side_effects=True),
     )(pair, ln_in_gain.reshape(1, 128), ln_in_bias.reshape(1, 128), w_proj, w_gate,

time: 56 us -> 52.6 us (0.939)
  Pallas kernels: 53.4 us -> 51.5 us
  local copies, waits for them, and re-layouts: 2.36 us -> 1.02 us
    pallas_call x1, Pallas kernels: 53.4 us -> 51.5 us  [on_device(): pl.pallas_call(kernel, name='triangle', out_shape=pltpu.VMEM((24, 192, 12...]
    unnamed x1, local copies, waits for them, and re-layouts: 2.36 us -> 1.02 us
where the time goes in v4:
time: 52.6 us; the launch traced here: 52.5 us
  Pallas kernels  51.5 us (98%)
  local copies, waits for them, and re-layouts  1.02 us (2%)
    pallas_call x1, Pallas kernels, on_device(): pl.pallas_call(kernel, name='triangle', out_shape=pltpu.VMEM((24, 192, 12...  51.5 us

profile of v4, /device:TPU:0, one launch (start us, length us, event | category | flops | bytes accessed | tf_op | source)
XLA Modules:
  0.0 52.5 jit_solution(14338642762623539218)
XLA Ops:
  0.0 51.5 %triangle.1 = bf16[24,192,128]{2,1,0:T(8,128)(2,1)S(1)} custom-call(bf16[24,192,128]{2,1,0:T(8,128)(2,1)} %pair_hbm.1, f32[1,128]{1,0:T(1,128)} %bitcast.4, f32[1,128]{1,0:T(1,128)} %bitcast.5, bf16[128,512]{1,0:T(8,128)(2,1)} %w_hbm.1, bf16[128,128]{1,0:T(8,128)(2,1)} %wg_hbm.1, f32[1,128]{1,0:T(1,128)} %bitcast.6, f32[1,128]{1,0:T(1,128)} %bitcast.7, ...), custom_call_target="tpu_custom_call" | custom-call | tf_op jit(solution)/shard_map/triangle/pallas_call | solution.py:314
  51.5 1.0 %copy.10 = bf16[24,192,128]{2,1,0:T(8,128)(2,1)} copy(bf16[24,192,128]{2,1,0:T(8,128)(2,1)S(1)} %triangle.1) | data formatting | bytes 2359296

commit v5 on v4

--- a/solution.py
+++ b/solution.py
@@ -19,18 +19,13 @@
 
 
 FAR_FIRST = sorted(range(1, CHIPS), key=lambda o: (-distance(o), o * 21 % CHIPS))
+MIXED = [o * 21 % CHIPS for o in range(1, CHIPS)]
 
 
 def normalize(values, gain, bias):
     center = values - jnp.mean(values, axis=-1, keepdims=True)
     spread = jnp.mean(center * center, axis=-1, keepdims=True)
     return center * lax.rsqrt(spread + epsilon) * gain + bias
-
-
-def over_channels(ends, mid):
-    ends = jnp.sum(ends, axis=0)
-    mid = jnp.sum(mid, axis=0)
-    return ends * (1.0 / 128), (mid + pltpu.roll(mid, 64, 1)) * (1.0 / 128)
 
 
 def kernel(pair_hbm, gain_hbm, bias_hbm, w_hbm, wg_hbm, out_gain_hbm, out_bias_hbm, wo_hbm, out_ref,
@@ -70,24 +65,24 @@
     y_his = [v // 2 for v in ys]
     y_los = [v % 2 for v in ys]
 
-    def each_peer(act):
-        for o in FAR_FIRST:
+    def each_peer(act, order):
+        for o in order:
             dy = o // 4 % 4
             t_row = xs[o // 16] + zs[o % 4] + y_los[dy]
             act(y_his[dy] * 32 + t_row, (t_row, y_his[dy] * 2 + core))
 
-    def send(src, dst, send_sem, recv_sem):
+    def send(src, dst, send_sem, recv_sem, order=MIXED):
         def act(chip, device):
             pltpu.make_async_remote_copy(
                 src(chip), dst, send_sem, recv_sem, device_id=device, device_id_type=MESH
             ).start()
 
-        each_peer(act)
+        each_peer(act, order)
         pltpu.make_async_copy(src(me), dst, recv_sem).start()
 
     barrier = pltpu.get_barrier_semaphore()
     each_peer(lambda chip, device: pl.semaphore_signal(
-        barrier, inc=1, device_id=device, device_id_type=MESH))
+        barrier, inc=1, device_id=device, device_id_type=MESH), FAR_FIRST)
     pl.semaphore_signal(barrier, inc=1, device_id=twin, device_id_type=MESH)
 
     def flip(side):
@@ -163,8 +158,6 @@
              recv_r.at[part])
         return carry
 
-    lax.fori_loop(0, 3, send_right, 0)
-
     for copy in loads[3:]:
         copy.wait()
 
@@ -172,7 +165,13 @@
         gate[k] = jax.nn.sigmoid(jnp.dot(normed[k], wg_ref[...], preferred_element_type=f32))
         return carry
 
-    lax.fori_loop(0, 24, open_gate, 0)
+    def open_gates():
+        lax.fori_loop(0, 24, open_gate, 0)
+
+    pl.when(core == 1)(open_gates)
+    lax.fori_loop(0, 3, send_right, 0)
+    pl.when(core == 0)(open_gates)
+
 
     diagonal = (lax.broadcasted_iota(jnp.int32, (128, 128), 0)
                 == lax.broadcasted_iota(jnp.int32, (128, 128), 1))
@@ -255,7 +254,7 @@
 
     def send_last(it, carry):
         send(lambda chip: sent_t.at[2, chip, it], got_t.at[2, me, it], send_t.at[2],
-             recv_last.at[it])
+             recv_last.at[it], FAR_FIRST)
         return carry
 
     lax.fori_loop(0, 3, send_last, 0)
@@ -263,35 +262,22 @@
     for part in range(2):
         pltpu.make_async_copy(sent_t.at[part], got_t.at[part], recv_t.at[part]).wait()
 
-    def finish(it, carry):
-        pltpu.make_async_copy(sent_t.at[2, :, it], got_t.at[2, :, it], recv_last.at[it]).wait()
-        t0, mid, t2 = [got_t[part, :, it].astype(f32) for part in range(3)]
-        ends_mean, mid_mean = over_channels(t0 + t2, mid)
-        t0 = t0 - ends_mean[None]
-        t2 = t2 - ends_mean[None]
-        mid = mid - mid_mean[None]
-        ends_spread, mid_spread = over_channels(t0 * t0 + t2 * t2, mid * mid)
-        ends_root = lax.rsqrt(ends_spread + epsilon)[None]
-        mid_root = lax.rsqrt(mid_spread + epsilon)[None]
-        mixing[0] = (t0 * ends_root).reshape(512, 128)
-        mixing[1] = (mid * mid_root).reshape(512, 128)
-        mixing[2] = (t2 * ends_root).reshape(512, 128)
+    def mixed(part, i):
+        return mixing[part, pl.ds(i, 64, stride=8), :] * scale[part] + shift[part]
+
+    def mean_of(values):
+        total = jnp.sum(values, axis=0)
+        return (total + pltpu.roll(total, 64, 1)) * (1.0 / 128)
+
+    def finish_middle(it, carry):
+        t = got_t[1, :, it].astype(f32)
+        t = t - mean_of(t)[None]
+        mixing[1] = (t * lax.rsqrt(mean_of(t * t) + epsilon)[None]).reshape(512, 128)
         w = wo_ref[...]
         for pair in range(4):
-            mids = []
-            for n in range(2):
-                i = 2 * pair + n
-                mixed = [
-                    mixing[part, pl.ds(i, 64, stride=8), :] * scale[part] + shift[part]
-                    for part in range(3)
-                ]
-                mids.append(mixed[1])
-                ends = jnp.concatenate([mixed[0], mixed[2]], axis=0).astype(bf16)
-                result = lax.dot_general(ends, w, TN, preferred_element_type=f32)
-                k = 8 * it + i
-                out_ref[k, 0:128] = (gate[k, 0:128] * result).astype(bf16)
-            top = jnp.where(lane64 < 64, mids[0], pltpu.roll(mids[1], 64, 1))
-            low = jnp.where(lane64 < 64, pltpu.roll(mids[0], 64, 1), mids[1])
+            even, odd = mixed(1, 2 * pair), mixed(1, 2 * pair + 1)
+            top = jnp.where(lane64 < 64, even, pltpu.roll(odd, 64, 1))
+            low = jnp.where(lane64 < 64, pltpu.roll(even, 64, 1), odd)
             both = jnp.concatenate([top, low], axis=0).astype(bf16)
             result = lax.dot_general(both, w, TN, preferred_element_type=f32)
             for n in range(2):
@@ -299,7 +285,26 @@
                 out_ref[k, 128:192] = (gate[k, 128:192] * result[64 * n:64 * n + 64]).astype(bf16)
         return carry
 
-    lax.fori_loop(0, 3, finish, 0)
+    lax.fori_loop(0, 3, finish_middle, 0)
+
+    def finish_ends(it, carry):
+        pltpu.make_async_copy(sent_t.at[2, :, it], got_t.at[2, :, it], recv_last.at[it]).wait()
+        t0, t2 = [got_t[part, :, it].astype(f32) for part in (0, 2)]
+        mean = (jnp.sum(t0 + t2, axis=0) * (1.0 / 128))[None]
+        t0 = t0 - mean
+        t2 = t2 - mean
+        root = lax.rsqrt(jnp.sum(t0 * t0 + t2 * t2, axis=0) * (1.0 / 128) + epsilon)[None]
+        mixing[0] = (t0 * root).reshape(512, 128)
+        mixing[2] = (t2 * root).reshape(512, 128)
+        w = wo_ref[...]
+        for i in range(8):
+            ends = jnp.concatenate([mixed(0, i), mixed(2, i)], axis=0).astype(bf16)
+            result = lax.dot_general(ends, w, TN, preferred_element_type=f32)
+            k = 8 * it + i
+            out_ref[k, 0:128] = (gate[k, 0:128] * result).astype(bf16)
+        return carry
+
+    lax.fori_loop(0, 3, finish_ends, 0)
 
     most = pl.ds(0, CHIPS - 1)
     pltpu.make_async_copy(sent_l.at[most], own.at[most], send_l).wait()

time: 52.6 us -> 52.1 us (level)
  Pallas kernels: 51.5 us -> 50.9 us
    pallas_call x1, Pallas kernels: 51.5 us -> 50.9 us  [on_device(): pl.pallas_call(kernel, name='triangle', out_shape=pltpu.VMEM((24, 192, 12...]
where the time goes in v5:
time: 52.1 us; the launch traced here: 51.9 us
  Pallas kernels  50.9 us (98%)
  local copies, waits for them, and re-layouts  1.02 us (2%)
    pallas_call x1, Pallas kernels, on_device(): pl.pallas_call(kernel, name='triangle', out_shape=pltpu.VMEM((24, 192, 12...  50.9 us

profile of v5, /device:TPU:0, one launch (start us, length us, event | category | flops | bytes accessed | tf_op | source)
XLA Modules:
  0.0 51.9 jit_solution(5380002753954367896)
XLA Ops:
  0.0 50.9 %triangle.1 = bf16[24,192,128]{2,1,0:T(8,128)(2,1)S(1)} custom-call(bf16[24,192,128]{2,1,0:T(8,128)(2,1)} %pair_hbm.1, f32[1,128]{1,0:T(1,128)} %bitcast.4, f32[1,128]{1,0:T(1,128)} %bitcast.5, bf16[128,512]{1,0:T(8,128)(2,1)} %w_hbm.1, bf16[128,128]{1,0:T(8,128)(2,1)} %wg_hbm.1, f32[1,128]{1,0:T(1,128)} %bitcast.6, f32[1,128]{1,0:T(1,128)} %bitcast.7, ...), custom_call_target="tpu_custom_call" | custom-call | tf_op jit(solution)/shard_map/triangle/pallas_call | solution.py:319
  50.9 1.0 %copy.10 = bf16[24,192,128]{2,1,0:T(8,128)(2,1)} copy(bf16[24,192,128]{2,1,0:T(8,128)(2,1)S(1)} %triangle.1) | data formatting | bytes 2359296

commit v6 on v5

--- a/solution.py
+++ b/solution.py
@@ -31,7 +31,7 @@
 def kernel(pair_hbm, gain_hbm, bias_hbm, w_hbm, wg_hbm, out_gain_hbm, out_bias_hbm, wo_hbm, out_ref,
            pair_ref, gain_ref, bias_ref, w_ref, wg_ref, out_gain_ref, out_bias_ref, wo_ref,
            wide, tall, normed, gate, major, sent_l, sent_r, own, other, right, turned, sent_t, got_t,
-           scale, shift, mixing,
+           scale, shift, mixing, half_mean, half_spread,
            load, load_pair, send_l, recv_l, pass_send, pass_recv, send_r, recv_r, send_t, recv_t, recv_last):
     def rows_of(kc):
         rows = pl.ds(pl.multiple_of(kc * 8, 8), 8)
@@ -283,6 +283,11 @@
             for n in range(2):
                 k = 8 * it + 2 * pair + n
                 out_ref[k, 128:192] = (gate[k, 128:192] * result[64 * n:64 * n + 64]).astype(bf16)
+        t0 = got_t[0, :, it].astype(f32)
+        mean = jnp.sum(t0, axis=0) * (1.0 / 64)
+        t0 = t0 - mean[None]
+        half_mean[it] = mean
+        half_spread[it] = jnp.sum(t0 * t0, axis=0)
         return carry
 
     lax.fori_loop(0, 3, finish_middle, 0)
@@ -290,10 +295,15 @@
     def finish_ends(it, carry):
         pltpu.make_async_copy(sent_t.at[2, :, it], got_t.at[2, :, it], recv_last.at[it]).wait()
         t0, t2 = [got_t[part, :, it].astype(f32) for part in (0, 2)]
-        mean = (jnp.sum(t0 + t2, axis=0) * (1.0 / 128))[None]
+        low = half_mean[it]
+        high = jnp.sum(t2, axis=0) * (1.0 / 64)
+        apart = t2 - high[None]
+        spread = half_spread[it] + jnp.sum(apart * apart, axis=0)
+        spread = (spread + (high - low) * (high - low) * 32.0) * (1.0 / 128)
+        root = lax.rsqrt(spread + epsilon)[None]
+        mean = ((low + high) * 0.5)[None]
         t0 = t0 - mean
         t2 = t2 - mean
-        root = lax.rsqrt(jnp.sum(t0 * t0 + t2 * t2, axis=0) * (1.0 / 128) + epsilon)[None]
         mixing[0] = (t0 * root).reshape(512, 128)
         mixing[2] = (t2 * root).reshape(512, 128)
         w = wo_ref[...]
@@ -347,6 +357,8 @@
             pltpu.VMEM((3, 64, 128), f32),
             pltpu.VMEM((3, 64, 128), f32),
             pltpu.VMEM((3, 512, 128), f32),
+            pltpu.VMEM((3, 8, 128), f32),
+            pltpu.VMEM((3, 8, 128), f32),
             dma((7,)), dma((3,)), dma, dma((3,)), dma((3,)), dma((3,)), dma((3,)), dma((3,)), dma((3,)), dma((3,)), dma((3,)),
         ],
         compiler_params=pltpu.CompilerParams(collective_id=0, has_side_effects=True),

time: 52.1 us -> 52.1 us (level)
  no operation moved by 1% of the time
where the time goes in v6:
time: 52.1 us; the launch traced here: 52 us
  Pallas kernels  50.9 us (98%)
  local copies, waits for them, and re-layouts  1.02 us (2%)
    pallas_call x1, Pallas kernels, on_device(): pl.pallas_call(kernel, name='triangle', out_shape=pltpu.VMEM((24, 192, 12...  50.9 us

profile of v6, /device:TPU:0, one launch (start us, length us, event | category | flops | bytes accessed | tf_op | source)
XLA Modules:
  0.0 52.0 jit_solution(5513889395160712048)
XLA Ops:
  0.0 50.9 %triangle.1 = bf16[24,192,128]{2,1,0:T(8,128)(2,1)S(1)} custom-call(bf16[24,192,128]{2,1,0:T(8,128)(2,1)} %pair_hbm.1, f32[1,128]{1,0:T(1,128)} %bitcast.4, f32[1,128]{1,0:T(1,128)} %bitcast.5, bf16[128,512]{1,0:T(8,128)(2,1)} %w_hbm.1, bf16[128,128]{1,0:T(8,128)(2,1)} %wg_hbm.1, f32[1,128]{1,0:T(1,128)} %bitcast.6, f32[1,128]{1,0:T(1,128)} %bitcast.7, ...), custom_call_target="tpu_custom_call" | custom-call | tf_op jit(solution)/shard_map/triangle/pallas_call | solution.py:329
  50.9 1.0 %copy.10 = bf16[24,192,128]{2,1,0:T(8,128)(2,1)} copy(bf16[24,192,128]{2,1,0:T(8,128)(2,1)S(1)} %triangle.1) | data formatting | bytes 2359296
